TPU v7x, 32 devices: a whole 2x2x4 slice. The times are simulated.
32 devices in a mesh: pairs: 2 (over x), src: 8 (over z, y), tgt: 2 (over core).
Axes of the slice: x: 2, y: 2, z: 4, core: 2. Of those that a mesh axis runs over, the one named last changes fastest.
Arguments:
- src_feat: float32 [2048, 32], P(('pairs', 'src'), 'tgt'), parts along dimension 0, may hold values from -0.72 to 0.72
- tgt_feat: float32 [32768, 32], P(('pairs', 'tgt'), 'src'), parts along dimension 0, may hold values from -0.72 to 0.72
- tgt_dual: float32 [32768], P(('pairs', 'tgt')), parts along dimension 0, may hold values from -6 to 6
- core_matrix: float32 [68, 34], P('pairs'), parts along dimension 0, may hold values from -3 to 3
Outputs:
- src_dual: float32 [2048], P(('pairs', 'src')), parts along dimension 0
- tgt_dual_out: float32 [32768], P(('pairs', 'tgt')), parts along dimension 0
- core_out: float32 [68, 34], P('pairs'), parts along dimension 0
There are 2 independent parts, one for each index of `pairs`. A program takes and returns all parts, laid end to end along the dimension named above; each array names one. Nothing has to cross between parts.
All inputs are finite; a program needn't handle non-finite values.
Results may differ from a plain program's by a relative error of at most 0.0003.
Values sent between devices are 32-bit elements; how exact they have to be, the bound alone decides.
No kernel may reach another device: no remote copies, remote signals or barrier semaphores. Data moves between devices by JAX's collectives and lax.ppermute only.
A program may use at most 64 MiB of HBM per device.

v0:
```python
import jax
import jax.numpy as jnp
from jax import lax
from jax.sharding import PartitionSpec as P

OUTER = 2
EPSILON = 0.02
HIGH = lax.Precision.HIGHEST


def merged(array, axis, combine):
    everything = jax.tree.map(lambda part: lax.all_gather(part, axis), array)
    leading = jax.tree.map(lambda part: part[0], everything)

    def step(k, so_far):
        return combine(so_far, jax.tree.map(lambda part: part[k], everything))

    return lax.fori_loop(1, lax.axis_size(axis), step, leading)


def lifted(values):
    squares = jnp.sum(values * values, axis=1, keepdims=True)
    ones = jnp.ones_like(squares)
    left = jnp.concatenate([squares, ones, -2.0 * values], axis=1)
    right = jnp.concatenate([ones, squares, values], axis=1)
    return (left, right)


def merge_logsum(earlier, later):
    top = jnp.maximum(earlier[0], later[0])
    return (top, earlier[1] * jnp.exp(earlier[0] - top) + later[1] * jnp.exp(later[0] - top))


def shards(src_feat, tgt_feat, tgt_dual, core_matrix):
    src_rows = lax.all_gather(src_feat, "tgt", axis=1, tiled=True)
    tgt_rows = lax.all_gather(tgt_feat, "src", axis=1, tiled=True)
    src_left, src_right = lifted(src_rows)
    tgt_left, tgt_right = lifted(tgt_rows)
    src_count = lax.axis_size("src")
    tgt_count = lax.axis_size("tgt")
    row_count = src_rows.shape[0]
    col_count = tgt_rows.shape[0]
    log_src = -jnp.log(jnp.float32(row_count * src_count))
    log_tgt = -jnp.log(jnp.float32(col_count * tgt_count))
    src_dual = jnp.zeros((row_count,), jnp.float32)
    for outer_step in range(OUTER):
        projected = jnp.dot(src_left, core_matrix, precision=HIGH)
        linear = jnp.dot(projected, tgt_right.T, precision=HIGH)
        row_logits = (tgt_dual[None, :] - linear) / EPSILON
        row_max = jnp.max(row_logits, axis=1)
        row_total = jnp.sum(jnp.exp(row_logits - row_max[:, None]), axis=1)
        row_max, row_total = merged((row_max, row_total), "tgt", merge_logsum)
        src_dual = EPSILON * log_src - EPSILON * (row_max + jnp.log(row_total))
        col_logits = (src_dual[:, None] - linear) / EPSILON
        col_max = jnp.max(col_logits, axis=0)
        col_exp = jnp.exp(col_logits - col_max[None, :])
        col_total = jnp.sum(col_exp, axis=0)
        piece_max, piece_total = (
            lax.all_to_all(col_max[None, :], "src", split_axis=1, concat_axis=0, tiled=True),
            lax.all_to_all(col_total[None, :], "src", split_axis=1, concat_axis=0, tiled=True),
        )
        whole_max = jnp.max(piece_max, axis=0)
        whole_total = jnp.sum(piece_total * jnp.exp(piece_max - whole_max[None, :]), axis=0)
        dual_piece = EPSILON * log_tgt - EPSILON * (whole_max + jnp.log(whole_total))
        tgt_dual = lax.all_gather(dual_piece, "src", axis=0, tiled=True)
        coupling = jnp.exp((src_dual[:, None] + tgt_dual[None, :] - linear) / EPSILON)
        weighted = jnp.dot(coupling, tgt_left, precision=HIGH)
        core_part = jnp.dot(src_right.T, weighted, precision=HIGH)
        core_matrix = -2.0 * lax.psum(core_part, ("src", "tgt"))
    return (src_dual, tgt_dual, core_matrix)


def solution(mesh):
    placed = (
        P(("pairs", "src"), "tgt"),
        P(("pairs", "tgt"), "src"),
        P(("pairs", "tgt")),
        P("pairs", None),
    )
    return jax.shard_map(
        shards,
        mesh=mesh,
        in_specs=placed,
        out_specs=(P(("pairs", "src")), P(("pairs", "tgt")), P("pairs", None)),
        check_vma=False,
    )
```

profile of v0, /device:TPU:0, one launch (start us, length us, event | category | flops | bytes accessed | tf_op | source)
XLA Modules:
  0.0 312.0 jit_solution(1951934580604606527)
XLA Ops:
  7.2 0.7 all-gather.11.cloned.1.call-update
  7.9 2.2 all_gather.36
  10.4 42.7 %all-gather.11.cloned.1.call-done = f32[8,4,8192]{2,1,0:T(4,128)} async-done(((f32[1,4,8192]{2,1,0:T(4,128)}), f32[8,4,8192]{2,1,0:T(4,128)}) %all-gather.11.cloned.1.call-update) | async-done | bytes 1048592 | tf_op jit(solution)/shard_map/all_gather | solution.py:36
  53.2 1.6 reshape.132
  55.0 3.8 %fusion.10 = (f32[128]{0:T(128)S(1)}, f32[128,8192]{1,0:T(8,128)S(1)}) fusion(f32[8192]{0:T(1024)S(1)} %copy-done.3, f32[128,34]{1,0:T(8,128)S(1)} %fusion.32, f32[8192,32]{0,1:T(8,128)S(1)} %bitcast.89, f32[8192,1]{0,1:T(1,128)S(1)} %bitcast.91, f32[8192,1]{0,1:T(1,128)S(1)} %broadcast_in_dim.10), kind=kOutput, calls=%fused_computation.18 | convolution fusion | flops 431521664 | bytes 5359104 | tf_op jit(solution)/shard_map/dot_general | solution.py:48
  58.8 1.0 exponential_reduce_fusion.3
  59.8 1.8 all-gather.6
  61.6 1.8 all-gather.5
  63.4 1.2 fusion.11
  64.5 3.3 %all-to-all-start = ((f32[1,8,1024]{2,0,1:T(1,128)}), f32[1,8,1024]{2,0,1:T(1,128)S(1)}, u32[]{:S(2)}, u32[]{:S(2)}) async-start(f32[1,8,1024]{2,0,1:T(1,128)} %bitcast.11), calls=%async_computation | async-start | bytes 65536 | tf_op jit(solution)/shard_map/all_to_all | solution.py:59
  67.9 3.7 %exponential_reduce_fusion.2 = f32[8192]{0:T(1024)} fusion(f32[128,8192]{1,0:T(8,128)} %copy-done.2, f32[8192]{0:T(1024)} %fusion.11, f32[128]{0:T(128)S(1)} %multiply_subtract_fusion.3), kind=kLoop, calls=%fused_computation.14 | loop fusion | flops 4186112 | bytes 4260352 | tf_op jit(solution)/shard_map/reduce_sum | solution.py:57
  71.6 2.9 all-to-all-done
  74.6 3.3 %all-to-all-start.1 = ((f32[1,8,1024]{2,0,1:T(1,128)}), f32[1,8,1024]{2,0,1:T(1,128)S(1)}, u32[]{:S(2)}, u32[]{:S(2)}) async-start(f32[1,8,1024]{2,0,1:T(1,128)} %bitcast.12), calls=%async_computation.1 | async-start | bytes 65536 | tf_op jit(solution)/shard_map/all_to_all | solution.py:60
  77.9 6.6 %all-to-all-done.1 = f32[1,8,1024]{2,0,1:T(1,128)S(1)} async-done(((f32[1,8,1024]{2,0,1:T(1,128)}), f32[1,8,1024]{2,0,1:T(1,128)S(1)}, u32[]{:S(2)}, u32[]{:S(2)}) %all-to-all-start.1) | async-done | bytes 32800 | tf_op jit(solution)/shard_map/all_to_all | solution.py:60
  84.6 30.6 %all_gather.42 = f32[8192]{0:T(1024)S(1)} all-gather(f32[1024]{0:T(1024)S(1)} %multiply_subtract_fusion.1), channel_id=1, replica_groups=mesh['pairs'=2,'src'=8,'tgt'=2] {'src'}, dimensions={0}, use_global_device_ids=true | all-gather | bytes 36864 | tf_op jit(solution)/shard_map/all_gather | solution.py:65
  115.2 6.2 %fusion.5 = f32[128,34]{1,0:T(8,128)S(1)} fusion(f32[128,8192]{1,0:T(8,128)} %copy-done.2, f32[8192]{0:T(1024)S(1)} %all_gather.42, f32[128]{0:T(128)S(1)} %multiply_subtract_fusion.3, f32[8192,32]{0,1:T(8,128)S(1)} %get-tuple-element.27, f32[8192,1]{0,1:T(1,128)S(1)} %broadcast_in_dim.10, f32[8192,1]{0,1:T(1,128)S(1)} %bitcast.92), kind=kOutput, calls=%fused_computation.9 | convolution fusion | flops 431521792 | bytes 5359104 | tf_op jit(solution)/shard_map/dot_general | solution.py:67
  121.6 57.8 %psum.14 = f32[34,34]{1,0:T(8,128)S(1)} all-reduce(f32[34,34]{1,0:T(8,128)S(1)} %fusion.31), channel_id=1, replica_groups=mesh['pairs'=2,'src'=8,'tgt'=2] {'src','tgt'}, use_global_device_ids=true, to_apply=%region_8.0 | all-reduce | flops 1156 | bytes 9248 | tf_op jit(solution)/shard_map/psum | solution.py:69
  179.7 3.8 %fusion.12 = (f32[128]{0:T(128)S(1)}, f32[128,8192]{1,0:T(8,128)S(1)}) fusion(f32[8192]{0:T(1024)S(1)} %all_gather.42, f32[128,34]{1,0:T(8,128)S(1)} %fusion.28, f32[8192,32]{0,1:T(8,128)S(1)} %bitcast.90, f32[8192,1]{0,1:T(1,128)S(1)} %bitcast.93, f32[8192,1]{0,1:T(1,128)S(1)} %broadcast_in_dim.10), kind=kOutput, calls=%fused_computation.20 | convolution fusion | flops 431521664 | bytes 5359104 | tf_op jit(solution)/shard_map/dot_general | solution.py:48
  183.5 1.0 exponential_reduce_fusion.1
  184.5 1.8 all-gather.8
  186.3 1.8 all-gather.7
  188.1 1.1 fusion.13
  189.3 3.3 %all-to-all-start.2 = ((f32[1,8,1024]{2,0,1:T(1,128)}), f32[1,8,1024]{2,0,1:T(1,128)S(1)}, u32[]{:S(2)}, u32[]{:S(2)}) async-start(f32[1,8,1024]{2,0,1:T(1,128)} %bitcast.19), calls=%async_computation.2 | async-start | bytes 65536 | tf_op jit(solution)/shard_map/all_to_all | solution.py:59
  192.6 3.7 %exponential_reduce_fusion = f32[8192]{0:T(1024)} fusion(f32[128,8192]{1,0:T(8,128)} %copy-done.1, f32[8192]{0:T(1024)} %fusion.13, f32[128]{0:T(128)S(1)} %multiply_subtract_fusion.2), kind=kLoop, calls=%fused_computation.5 | loop fusion | flops 4186112 | bytes 4260352 | tf_op jit(solution)/shard_map/reduce_sum | solution.py:57
  196.4 2.9 all-to-all-done.2
  199.3 3.3 %all-to-all-start.3 = ((f32[1,8,1024]{2,0,1:T(1,128)}), f32[1,8,1024]{2,0,1:T(1,128)S(1)}, u32[]{:S(2)}, u32[]{:S(2)}) async-start(f32[1,8,1024]{2,0,1:T(1,128)} %bitcast.20), calls=%async_computation.3 | async-start | bytes 65536 | tf_op jit(solution)/shard_map/all_to_all | solution.py:60
  202.7 6.6 %all-to-all-done.3 = f32[1,8,1024]{2,0,1:T(1,128)S(1)} async-done(((f32[1,8,1024]{2,0,1:T(1,128)}), f32[1,8,1024]{2,0,1:T(1,128)S(1)}, u32[]{:S(2)}, u32[]{:S(2)}) %all-to-all-start.3) | async-done | bytes 32800 | tf_op jit(solution)/shard_map/all_to_all | solution.py:60
  209.3 30.6 %all_gather.47 = f32[8192]{0:T(1024)S(1)} all-gather(f32[1024]{0:T(1024)S(1)} %multiply_subtract_fusion), channel_id=1, replica_groups=mesh['pairs'=2,'src'=8,'tgt'=2] {'src'}, dimensions={0}, use_global_device_ids=true | all-gather | bytes 36864 | tf_op jit(solution)/shard_map/all_gather | solution.py:65
  239.9 6.2 %fusion = f32[128,34]{1,0:T(8,128)S(1)} fusion(f32[128,8192]{1,0:T(8,128)} %copy-done.1, f32[8192]{0:T(1024)S(1)} %all_gather.47, f32[128]{0:T(128)S(1)} %multiply_subtract_fusion.2, f32[8192,32]{0,1:T(8,128)S(1)} %get-tuple-element.27, f32[8192,1]{0,1:T(1,128)S(1)} %broadcast_in_dim.10, f32[8192,1]{0,1:T(1,128)S(1)} %bitcast.94), kind=kOutput, calls=%fused_computation | convolution fusion | flops 431521792 | bytes 5359104 | tf_op jit(solution)/shard_map/dot_general | solution.py:67
  246.3 57.6 %psum.15 = f32[34,34]{1,0:T(8,128)S(1)} all-reduce(f32[34,34]{1,0:T(8,128)S(1)} %fusion.30), channel_id=1, replica_groups=mesh['pairs'=2,'src'=8,'tgt'=2] {'src','tgt'}, use_global_device_ids=true, to_apply=%region_15.0 | all-reduce | flops 1156 | bytes 9248 | tf_op jit(solution)/shard_map/psum | solution.py:69
  303.9 0.6 broadcast_multiply_fusion.1
  304.5 0.6 copy.16
  (27 shorter events, 1.4 us)
Async XLA Ops:
  7.2 3.0 copy-start
  7.2 47.8 %copy-start.3 = (f32[8192]{0:T(1024)S(1)}, f32[8192]{0:T(1024)}, u32[]{:S(2)}) copy-start(f32[8192]{0:T(1024)} %param.6) | copy-start | bytes 98308
  7.2 46.0 %all-gather.11.cloned.1.call-start = ((), (), s32[]{:S(2)}) async-start(), calls=%async_computation.4 | async-start | bytes 1179648 | tf_op jit(solution)/shard_map/all_gather | solution.py:36
  58.8 5.8 %copy-start.2 = (f32[128,8192]{1,0:T(8,128)}, f32[128,8192]{1,0:T(8,128)S(1)}, u32[]{:S(2)}) copy-start(f32[128,8192]{1,0:T(8,128)S(1)} %get-tuple-element.38) | copy-start | bytes 12582916
  64.5 10.0 %all-to-all-start = ((f32[1,8,1024]{2,0,1:T(1,128)}), f32[1,8,1024]{2,0,1:T(1,128)S(1)}, u32[]{:S(2)}, u32[]{:S(2)}) async-start(f32[1,8,1024]{2,0,1:T(1,128)} %bitcast.11), calls=%async_computation | async-start | bytes 65536 | tf_op jit(solution)/shard_map/all_to_all | solution.py:59
  74.6 10.0 %all-to-all-start.1 = ((f32[1,8,1024]{2,0,1:T(1,128)}), f32[1,8,1024]{2,0,1:T(1,128)S(1)}, u32[]{:S(2)}, u32[]{:S(2)}) async-start(f32[1,8,1024]{2,0,1:T(1,128)} %bitcast.12), calls=%async_computation.1 | async-start | bytes 65536 | tf_op jit(solution)/shard_map/all_to_all | solution.py:60
  183.5 5.8 %copy-start.1 = (f32[128,8192]{1,0:T(8,128)}, f32[128,8192]{1,0:T(8,128)S(1)}, u32[]{:S(2)}) copy-start(f32[128,8192]{1,0:T(8,128)S(1)} %get-tuple-element.40) | copy-start | bytes 12582916
  188.1 51.8 %copy-start.4 = (f32[128]{0:T(128)}, f32[128]{0:T(128)S(1)}, u32[]{:S(2)}) copy-start(f32[128]{0:T(128)S(1)} %multiply_subtract_fusion.2) | copy-start | bytes 1540
  189.3 10.0 %all-to-all-start.2 = ((f32[1,8,1024]{2,0,1:T(1,128)}), f32[1,8,1024]{2,0,1:T(1,128)S(1)}, u32[]{:S(2)}, u32[]{:S(2)}) async-start(f32[1,8,1024]{2,0,1:T(1,128)} %bitcast.19), calls=%async_computation.2 | async-start | bytes 65536 | tf_op jit(solution)/shard_map/all_to_all | solution.py:59
  199.3 10.0 %all-to-all-start.3 = ((f32[1,8,1024]{2,0,1:T(1,128)}), f32[1,8,1024]{2,0,1:T(1,128)S(1)}, u32[]{:S(2)}, u32[]{:S(2)}) async-start(f32[1,8,1024]{2,0,1:T(1,128)} %bitcast.20), calls=%async_computation.3 | async-start | bytes 65536 | tf_op jit(solution)/shard_map/all_to_all | solution.py:60
Sparse Core Ops, SparseCore 0:
  10.1 42.9 all-gather.10
where the time goes:
time: 313 us; the launch traced here: 312 us
  blocking collectives  186 us (59%)
  waiting for transfers between devices  62.4 us (20%)
  matrix products  21 us (7%)
  between operations  14.2 us (5%)
  starting transfers between devices  13.4 us (4%)
  other arithmetic  12.7 us (4%)
    psum x2, blocking collectives, shards(): core_matrix = -2.0 * lax.psum(core_part, ('src', 'tgt'))  115 us
    all_gather x2, blocking collectives, shards(): tgt_dual = lax.all_gather(dual_piece, 'src', axis=0, tiled=True)  61.2 us
    all_gather x1, waiting for transfers between devices, shards(): tgt_rows = lax.all_gather(tgt_feat, 'src', axis=1, tiled=True)  42.7 us
    all_to_all x2, waiting for transfers between devices, shards(): lax.all_to_all(col_total[None, :], 'src', split_axis=1, concat_axis=0, ti...  13.2 us
    dot_general x2, matrix products, shards(): weighted = jnp.dot(coupling, tgt_left, precision=HIGH)  12.4 us
    dot_general x2, matrix products, shards(): linear = jnp.dot(projected, tgt_right.T, precision=HIGH)  7.61 us
    reduce_sum x2, other arithmetic, shards(): col_total = jnp.sum(col_exp, axis=0)  7.45 us
    all_gather x4, blocking collectives, merged(): everything = jax.tree.map(lambda part: lax.all_gather(part, axis), array)  7.19 us
  transfers between devices with their start and end apart: 5, of which 5 were waited for; matrix products, arithmetic and copies ran while one was open for 3% of the time, Pallas kernels for 0%

commit v1 on v0

--- a/solution.py
+++ b/solution.py
@@ -66,7 +66,11 @@
         coupling = jnp.exp((src_dual[:, None] + tgt_dual[None, :] - linear) / EPSILON)
         weighted = jnp.dot(coupling, tgt_left, precision=HIGH)
         core_part = jnp.dot(src_right.T, weighted, precision=HIGH)
-        core_matrix = -2.0 * lax.psum(core_part, ("src", "tgt"))
+
+        def read_indices(page, row_axis):
+            return jax.lax.all_gather(page, axis_name=row_axis).sum(axis=0)
+
+        core_matrix = -2.0 * read_indices(core_part, row_axis=("src", "tgt"))
     return (src_dual, tgt_dual, core_matrix)
 
 

time: 313 us -> 235 us (0.75)
  blocking collectives: 186 us -> 108 us
    psum x2 -> x0, blocking collectives: 115 us -> none  [shards(): core_matrix = -2.0 * lax.psum(core_part, ('src', 'tgt'))]
    all_gather x0 -> x2, blocking collectives: none -> 37.4 us  [read_indices(): return jax.lax.all_gather(page, axis_name=row_axis).sum(axis=0)]
where the time goes in v1:
time: 235 us; the launch traced here: 234 us
  blocking collectives  108 us (46%)
  waiting for transfers between devices  62.4 us (27%)
  matrix products  21 us (9%)
  between operations  14.2 us (6%)
  starting transfers between devices  13.4 us (6%)
  other arithmetic  12.8 us (5%)
    all_gather x2, blocking collectives, shards(): tgt_dual = lax.all_gather(dual_piece, 'src', axis=0, tiled=True)  61.2 us
    all_gather x1, waiting for transfers between devices, shards(): tgt_rows = lax.all_gather(tgt_feat, 'src', axis=1, tiled=True)  42.7 us
    all_gather x2, blocking collectives, read_indices(): return jax.lax.all_gather(page, axis_name=row_axis).sum(axis=0)  37.4 us
    all_to_all x2, waiting for transfers between devices, shards(): lax.all_to_all(col_total[None, :], 'src', split_axis=1, concat_axis=0, ti...  13.2 us
    dot_general x2, matrix products, shards(): weighted = jnp.dot(coupling, tgt_left, precision=HIGH)  12.4 us
    dot_general x2, matrix products, shards(): linear = jnp.dot(projected, tgt_right.T, precision=HIGH)  7.61 us
    reduce_sum x2, other arithmetic, shards(): col_total = jnp.sum(col_exp, axis=0)  7.45 us
    all_gather x4, blocking collectives, merged(): everything = jax.tree.map(lambda part: lax.all_gather(part, axis), array)  7.19 us
  transfers between devices with their start and end apart: 5, of which 5 were waited for; matrix products, arithmetic and copies ran while one was open for 3% of the time, Pallas kernels for 0%

profile of v1, /device:TPU:0, one launch (start us, length us, event | category | flops | bytes accessed | tf_op | source)
XLA Modules:
  0.0 234.1 jit_solution(6377584103374106465)
XLA Ops:
  7.2 0.7 all-gather.15.cloned.1.call-update
  7.9 2.2 all_gather.48
  10.4 42.7 %all-gather.15.cloned.1.call-done = f32[8,4,8192]{2,1,0:T(4,128)} async-done(((f32[1,4,8192]{2,1,0:T(4,128)}), f32[8,4,8192]{2,1,0:T(4,128)}) %all-gather.15.cloned.1.call-update) | async-done | bytes 1048592 | tf_op jit(solution)/shard_map/all_gather | solution.py:36
  53.2 1.6 reshape.134
  55.0 3.8 %fusion.10 = (f32[128]{0:T(128)S(1)}, f32[128,8192]{1,0:T(8,128)S(1)}) fusion(f32[8192]{0:T(1024)S(1)} %copy-done.3, f32[128,34]{1,0:T(8,128)S(1)} %fusion.30, f32[8192,32]{0,1:T(8,128)S(1)} %bitcast.93, f32[8192,1]{0,1:T(1,128)S(1)} %bitcast.95, f32[8192,1]{0,1:T(1,128)S(1)} %broadcast_in_dim.10), kind=kOutput, calls=%fused_computation.18 | convolution fusion | flops 431521664 | bytes 5359104 | tf_op jit(solution)/shard_map/dot_general | solution.py:48
  58.8 1.0 exponential_reduce_fusion.3
  59.8 1.8 all-gather.8
  61.6 1.8 all-gather.7
  63.4 1.2 fusion.11
  64.5 3.3 %all-to-all-start = ((f32[1,8,1024]{2,0,1:T(1,128)}), f32[1,8,1024]{2,0,1:T(1,128)S(1)}, u32[]{:S(2)}, u32[]{:S(2)}) async-start(f32[1,8,1024]{2,0,1:T(1,128)} %bitcast.11), calls=%async_computation | async-start | bytes 65536 | tf_op jit(solution)/shard_map/all_to_all | solution.py:59
  67.9 3.7 %exponential_reduce_fusion.2 = f32[8192]{0:T(1024)} fusion(f32[128,8192]{1,0:T(8,128)} %copy-done.2, f32[8192]{0:T(1024)} %fusion.11, f32[128]{0:T(128)S(1)} %multiply_subtract_fusion.3), kind=kLoop, calls=%fused_computation.14 | loop fusion | flops 4186112 | bytes 4260352 | tf_op jit(solution)/shard_map/reduce_sum | solution.py:57
  71.6 2.9 %all-to-all-done = f32[1,8,1024]{2,0,1:T(1,128)S(1)} async-done(((f32[1,8,1024]{2,0,1:T(1,128)}), f32[1,8,1024]{2,0,1:T(1,128)S(1)}, u32[]{:S(2)}, u32[]{:S(2)}) %all-to-all-start) | async-done | bytes 32800 | tf_op jit(solution)/shard_map/all_to_all | solution.py:59
  74.6 3.3 %all-to-all-start.1 = ((f32[1,8,1024]{2,0,1:T(1,128)}), f32[1,8,1024]{2,0,1:T(1,128)S(1)}, u32[]{:S(2)}, u32[]{:S(2)}) async-start(f32[1,8,1024]{2,0,1:T(1,128)} %bitcast.12), calls=%async_computation.1 | async-start | bytes 65536 | tf_op jit(solution)/shard_map/all_to_all | solution.py:60
  77.9 6.6 %all-to-all-done.1 = f32[1,8,1024]{2,0,1:T(1,128)S(1)} async-done(((f32[1,8,1024]{2,0,1:T(1,128)}), f32[1,8,1024]{2,0,1:T(1,128)S(1)}, u32[]{:S(2)}, u32[]{:S(2)}) %all-to-all-start.1) | async-done | bytes 32800 | tf_op jit(solution)/shard_map/all_to_all | solution.py:60
  84.6 30.6 %all_gather.54 = f32[8192]{0:T(1024)S(1)} all-gather(f32[1024]{0:T(1024)S(1)} %multiply_subtract_fusion.1), channel_id=1, replica_groups=mesh['pairs'=2,'src'=8,'tgt'=2] {'src'}, dimensions={0}, use_global_device_ids=true | all-gather | bytes 36864 | tf_op jit(solution)/shard_map/all_gather | solution.py:65
  115.2 6.2 %fusion.5 = f32[128,34]{1,0:T(8,128)S(1)} fusion(f32[128,8192]{1,0:T(8,128)} %copy-done.2, f32[8192]{0:T(1024)S(1)} %all_gather.54, f32[128]{0:T(128)S(1)} %multiply_subtract_fusion.3, f32[8192,32]{0,1:T(8,128)S(1)} %get-tuple-element.27, f32[8192,1]{0,1:T(1,128)S(1)} %broadcast_in_dim.10, f32[8192,1]{0,1:T(1,128)S(1)} %bitcast.96), kind=kOutput, calls=%fused_computation.9 | convolution fusion | flops 431521792 | bytes 5359104 | tf_op jit(solution)/shard_map/dot_general | solution.py:67
  121.6 18.8 %all-gather.9 = f32[16,34,34]{2,1,0:T(8,128)S(1)} all-gather(f32[1,34,34]{2,1,0:T(8,128)S(1)} %convolution_bitcast_fusion.1), channel_id=4, replica_groups=mesh['pairs'=2,'src'=8,'tgt'=2] {'src','tgt'}, dimensions={0}, use_global_device_ids=true | all-gather | bytes 78608 | tf_op jit(solution)/shard_map/all_gather | solution.py:71
  140.7 3.8 %fusion.12 = (f32[128]{0:T(128)S(1)}, f32[128,8192]{1,0:T(8,128)S(1)}) fusion(f32[8192]{0:T(1024)S(1)} %all_gather.54, f32[128,34]{1,0:T(8,128)S(1)} %fusion.28, f32[8192,32]{0,1:T(8,128)S(1)} %bitcast.94, f32[8192,1]{0,1:T(1,128)S(1)} %bitcast.97, f32[8192,1]{0,1:T(1,128)S(1)} %broadcast_in_dim.10), kind=kOutput, calls=%fused_computation.20 | convolution fusion | flops 431521664 | bytes 5359104 | tf_op jit(solution)/shard_map/dot_general | solution.py:48
  144.6 1.0 exponential_reduce_fusion.1
  145.6 1.8 all-gather.11
  147.4 1.8 all-gather.10
  149.2 1.1 fusion.13
  150.3 3.3 %all-to-all-start.2 = ((f32[1,8,1024]{2,0,1:T(1,128)}), f32[1,8,1024]{2,0,1:T(1,128)S(1)}, u32[]{:S(2)}, u32[]{:S(2)}) async-start(f32[1,8,1024]{2,0,1:T(1,128)} %bitcast.20), calls=%async_computation.2 | async-start | bytes 65536 | tf_op jit(solution)/shard_map/all_to_all | solution.py:59
  153.7 3.7 %exponential_reduce_fusion = f32[8192]{0:T(1024)} fusion(f32[128,8192]{1,0:T(8,128)} %copy-done.1, f32[8192]{0:T(1024)} %fusion.13, f32[128]{0:T(128)S(1)} %multiply_subtract_fusion.2), kind=kLoop, calls=%fused_computation.5 | loop fusion | flops 4186112 | bytes 4260352 | tf_op jit(solution)/shard_map/reduce_sum | solution.py:57
  157.4 2.9 %all-to-all-done.2 = f32[1,8,1024]{2,0,1:T(1,128)S(1)} async-done(((f32[1,8,1024]{2,0,1:T(1,128)}), f32[1,8,1024]{2,0,1:T(1,128)S(1)}, u32[]{:S(2)}, u32[]{:S(2)}) %all-to-all-start.2) | async-done | bytes 32800 | tf_op jit(solution)/shard_map/all_to_all | solution.py:59
  160.3 3.3 %all-to-all-start.3 = ((f32[1,8,1024]{2,0,1:T(1,128)}), f32[1,8,1024]{2,0,1:T(1,128)S(1)}, u32[]{:S(2)}, u32[]{:S(2)}) async-start(f32[1,8,1024]{2,0,1:T(1,128)} %bitcast.21), calls=%async_computation.3 | async-start | bytes 65536 | tf_op jit(solution)/shard_map/all_to_all | solution.py:60
  163.7 6.6 %all-to-all-done.3 = f32[1,8,1024]{2,0,1:T(1,128)S(1)} async-done(((f32[1,8,1024]{2,0,1:T(1,128)}), f32[1,8,1024]{2,0,1:T(1,128)S(1)}, u32[]{:S(2)}, u32[]{:S(2)}) %all-to-all-start.3) | async-done | bytes 32800 | tf_op jit(solution)/shard_map/all_to_all | solution.py:60
  170.3 30.6 %all_gather.61 = f32[8192]{0:T(1024)S(1)} all-gather(f32[1024]{0:T(1024)S(1)} %multiply_subtract_fusion), channel_id=1, replica_groups=mesh['pairs'=2,'src'=8,'tgt'=2] {'src'}, dimensions={0}, use_global_device_ids=true | all-gather | bytes 36864 | tf_op jit(solution)/shard_map/all_gather | solution.py:65
  200.9 6.2 %fusion = f32[128,34]{1,0:T(8,128)S(1)} fusion(f32[128,8192]{1,0:T(8,128)} %copy-done.1, f32[8192]{0:T(1024)S(1)} %all_gather.61, f32[128]{0:T(128)S(1)} %multiply_subtract_fusion.2, f32[8192,32]{0,1:T(8,128)S(1)} %get-tuple-element.27, f32[8192,1]{0,1:T(1,128)S(1)} %broadcast_in_dim.10, f32[8192,1]{0,1:T(1,128)S(1)} %bitcast.98), kind=kOutput, calls=%fused_computation | convolution fusion | flops 431521792 | bytes 5359104 | tf_op jit(solution)/shard_map/dot_general | solution.py:67
  207.3 18.6 %all-gather.12 = f32[16,34,34]{2,1,0:T(8,128)S(1)} all-gather(f32[1,34,34]{2,1,0:T(8,128)S(1)} %convolution_bitcast_fusion), channel_id=7, replica_groups=mesh['pairs'=2,'src'=8,'tgt'=2] {'src','tgt'}, dimensions={0}, use_global_device_ids=true | all-gather | bytes 78608 | tf_op jit(solution)/shard_map/all_gather | solution.py:71
  226.0 0.6 broadcast_multiply_fusion.1
  226.6 0.6 copy.16
  (29 shorter events, 1.5 us)
Async XLA Ops:
  7.2 3.0 %copy-start = (f32[34,34]{1,0:T(8,128)S(1)}, f32[34,34]{1,0:T(8,128)}, u32[]{:S(2)}) copy-start(f32[34,34]{1,0:T(8,128)} %param.7) | copy-start | bytes 13876
  7.2 47.8 %copy-start.3 = (f32[8192]{0:T(1024)S(1)}, f32[8192]{0:T(1024)}, u32[]{:S(2)}) copy-start(f32[8192]{0:T(1024)} %param.6) | copy-start | bytes 98308
  7.2 46.0 %all-gather.15.cloned.1.call-start = ((), (), s32[]{:S(2)}) async-start(), calls=%async_computation.4 | async-start | bytes 1179648 | tf_op jit(solution)/shard_map/all_gather | solution.py:36
  58.8 5.8 %copy-start.2 = (f32[128,8192]{1,0:T(8,128)}, f32[128,8192]{1,0:T(8,128)S(1)}, u32[]{:S(2)}) copy-start(f32[128,8192]{1,0:T(8,128)S(1)} %get-tuple-element.38) | copy-start | bytes 12582916
  64.5 10.0 %all-to-all-start = ((f32[1,8,1024]{2,0,1:T(1,128)}), f32[1,8,1024]{2,0,1:T(1,128)S(1)}, u32[]{:S(2)}, u32[]{:S(2)}) async-start(f32[1,8,1024]{2,0,1:T(1,128)} %bitcast.11), calls=%async_computation | async-start | bytes 65536 | tf_op jit(solution)/shard_map/all_to_all | solution.py:59
  74.6 10.0 %all-to-all-start.1 = ((f32[1,8,1024]{2,0,1:T(1,128)}), f32[1,8,1024]{2,0,1:T(1,128)S(1)}, u32[]{:S(2)}, u32[]{:S(2)}) async-start(f32[1,8,1024]{2,0,1:T(1,128)} %bitcast.12), calls=%async_computation.1 | async-start | bytes 65536 | tf_op jit(solution)/shard_map/all_to_all | solution.py:60
  144.5 5.8 %copy-start.1 = (f32[128,8192]{1,0:T(8,128)}, f32[128,8192]{1,0:T(8,128)S(1)}, u32[]{:S(2)}) copy-start(f32[128,8192]{1,0:T(8,128)S(1)} %get-tuple-element.40) | copy-start | bytes 12582916
  149.2 51.8 %copy-start.4 = (f32[128]{0:T(128)}, f32[128]{0:T(128)S(1)}, u32[]{:S(2)}) copy-start(f32[128]{0:T(128)S(1)} %multiply_subtract_fusion.2) | copy-start | bytes 1540
  150.3 10.0 %all-to-all-start.2 = ((f32[1,8,1024]{2,0,1:T(1,128)}), f32[1,8,1024]{2,0,1:T(1,128)S(1)}, u32[]{:S(2)}, u32[]{:S(2)}) async-start(f32[1,8,1024]{2,0,1:T(1,128)} %bitcast.20), calls=%async_computation.2 | async-start | bytes 65536 | tf_op jit(solution)/shard_map/all_to_all | solution.py:59
  160.3 10.0 %all-to-all-start.3 = ((f32[1,8,1024]{2,0,1:T(1,128)}), f32[1,8,1024]{2,0,1:T(1,128)S(1)}, u32[]{:S(2)}, u32[]{:S(2)}) async-start(f32[1,8,1024]{2,0,1:T(1,128)} %bitcast.21), calls=%async_computation.3 | async-start | bytes 65536 | tf_op jit(solution)/shard_map/all_to_all | solution.py:60
Sparse Core Ops, SparseCore 0:
  10.1 42.9 all-gather.14
